TPU v7x, 128 devices: a whole 4x4x4 slice. The times are simulated.
128 devices in a mesh: seq: 64 (over x_lo, z, y, core), ch: 2 (over x_hi).
Axes of the slice: x: 4 (x_hi: 2, x_lo: 2; x = x_hi * 2 + x_lo), y: 4, z: 4, core: 2. Of those that a mesh axis runs over, the one named last changes fastest.
Arguments:
- inputs: bfloat16 [4, 16384, 1536], P(None, 'seq', 'ch'), may hold values from -6 to 6
- kernels: float32 [3, 3, 1536], P(None, None, 'ch'), may hold values from -3.5 to 3.5
- mixers: bfloat16 [3, 1536, 1536], P(None, None, 'ch'), may hold values from -0.15625 to 0.15625
- cotangent: bfloat16 [4, 16384, 1536], P(None, 'seq', 'ch'), may hold values from -6 to 6
Outputs:
- outputs: bfloat16 [4, 16384, 1536], P(None, 'seq', 'ch')
- input_grad: bfloat16 [4, 16384, 1536], P(None, 'seq', 'ch')
- mixer_grads: float32 [3, 1536, 1536], P(None, 'seq', 'ch')
All inputs are finite; a program needn't handle non-finite values.
Results may differ from a plain program's by a relative error of at most 0.0075.
Values may be sent and summed in bfloat16 or wider, within the bound.
A program may use at most 128 MiB of HBM per device.

v0:
```python
import math
import jax
import jax.numpy as jnp
from jax import lax
from jax.sharding import PartitionSpec as P

dilations = (2, 4, 8)


def padded_2(block, sides, width):
    for axis, dim in sides:
        count = lax.axis_size(axis)
        forward = [(i, i + 1) for i in range(count - 1)]
        backward = [(target, source) for source, target in forward]
        low = lax.ppermute(
            lax.slice_in_dim(block, block.shape[dim] - width, None, axis=dim), axis, forward
        )
        high = lax.ppermute(lax.slice_in_dim(block, 0, width, axis=dim), axis, backward)
        block = jnp.concatenate([low, block, high], axis=dim)
    return block


def gelu_exact(value):
    return 0.5 * value * (1.0 + jax.scipy.special.erf(value * 0.7071067811865476))


def gelu_slope(value):
    return (
        0.5 * (1.0 + jax.scipy.special.erf(value * 0.7071067811865476))
        + value * jnp.exp(-0.5 * value * value) * 0.3989422804014327
    )


def convolve(padded, kernel, width):
    length = padded.shape[1] - 2 * width
    wide = padded.astype(jnp.float32)
    return (
        kernel[0] * wide[:, 0:length]
        + kernel[1] * wide[:, width : width + length]
        + kernel[2] * wide[:, 2 * width : 2 * width + length]
    )


def mixing(center, act, mixer):
    seqs, length, chans = act.shape
    gathered = lax.all_gather(act.reshape(seqs * length, chans), "ch", axis=1, tiled=True)
    mixed = jnp.dot(gathered, mixer, preferred_element_type=jnp.float32)
    result = (center.astype(jnp.float32) + mixed.reshape(seqs, length, chans)).astype(jnp.bfloat16)
    return (gathered, result)


def on_device(inputs, kernels, mixers, cotangent):
    seqs, bins, chans = inputs.shape
    devices_seq = lax.axis_size("seq")
    saved = []
    current = inputs
    for block, width in enumerate(dilations):
        padded = padded_2(current, (("seq", 1),), width)
        pre = convolve(padded, kernels[block], width)
        act = gelu_exact(pre).astype(jnp.bfloat16)
        gathered, current = mixing(current, act, mixers[block])
        saved.append((pre, gathered))
    scale = 1.0 / math.sqrt(seqs * bins * devices_seq)
    grad_list = [None, None, None]
    upper = cotangent
    for block in (2, 1, 0):
        width = dilations[block]
        kernel = kernels[block]
        pre, gathered = saved[block]
        flat = upper.reshape(seqs * bins, chans)
        term = jnp.einsum("rj,cj->rc", flat, mixers[block], preferred_element_type=jnp.float32)
        back = lax.psum_scatter(term, "ch", scatter_dimension=1, tiled=True)
        slope = (back.reshape(seqs, bins, chans) * gelu_slope(pre)).astype(jnp.bfloat16)
        local_grad = (
            jnp.einsum("rc,rj->cj", gathered, flat, preferred_element_type=jnp.float32) * scale
        )
        grad_list[block] = local_grad
        padded = padded_2(slope, (("seq", 1),), width).astype(jnp.float32)
        lower = (
            upper.astype(jnp.float32)
            + kernel[0] * padded[:, 2 * width : 2 * width + bins]
            + kernel[1] * padded[:, width : width + bins]
            + kernel[2] * padded[:, 0:bins]
        )
        upper = lower.astype(jnp.bfloat16)
    mixer_grads = lax.psum_scatter(jnp.stack(grad_list), "seq", scatter_dimension=1, tiled=True)
    return (current, upper, mixer_grads)


def solution(mesh):
    placed = (P(None, "seq", "ch"), P(None, None, "ch"), P(None, None, "ch"), P(None, "seq", "ch"))
    return jax.shard_map(
        on_device,
        mesh=mesh,
        in_specs=placed,
        out_specs=(P(None, "seq", "ch"), P(None, "seq", "ch"), P(None, "seq", "ch")),
        check_vma=False,
    )
```

profile of v0, /device:TPU:0, one launch (start us, length us, event | category | flops | bytes accessed | tf_op | source)
XLA Modules:
  0.0 783.3 jit_solution(2955091546215567638)
XLA Ops:
  7.2 0.0 all-gather.4.cloned.1.call-start
  7.2 0.8 fusion.68
  8.1 1.3 collective-permute-start.1
  9.4 3.0 collective-permute-start
  12.4 0.9 slice_reduce_fusion.2
  13.4 1.8 maximum_convert_fusion.2
  15.1 2.9 multiply_convert_fusion.2
  18.1 0.0 all-gather.4.cloned.1.call-update
  18.1 0.0 all-gather.6.cloned.1.call-start
  18.2 57.2 %all-gather.4.cloned.1.call-done = bf16[1024,1536]{1,0:T(8,128)(2,1)} async-done(((bf16[1024,768]{1,0:T(8,128)(2,1)}), bf16[1024,1536]{1,0:T(8,128)(2,1)}) %all-gather.4.cloned.1.call-update) | async-done | bytes 3145744 | tf_op jit(solution)/shard_map/all_gather | solution.py:46
  75.4 5.2 add_convert_fusion.2
  80.6 1.3 collective-permute-start.3
  81.9 3.0 collective-permute-start.2
  85.0 0.8 collective-permute-done.2
  85.8 0.3 maximum_convert_fusion.3
  86.1 2.9 multiply_convert_fusion.1
  89.0 0.0 all-gather.6.cloned.1.call-update
  89.0 0.0 reduce-scatter.5.cloned.1.call-start
  89.1 6.2 fusion.38
  95.3 0.0 reduce-scatter.7.cloned.1.call-start
  95.4 48.2 %all-gather.6.cloned.1.call-done = bf16[1024,1536]{1,0:T(8,128)(2,1)} async-done(((bf16[1024,768]{1,0:T(8,128)(2,1)}), bf16[1024,1536]{1,0:T(8,128)(2,1)}) %all-gather.6.cloned.1.call-update) | async-done | bytes 3145744 | tf_op jit(solution)/shard_map/all_gather | solution.py:46
  143.5 5.2 add_convert_fusion.1
  148.8 1.3 collective-permute-start.5
  150.1 3.0 collective-permute-start.4
  153.1 0.9 collective-permute-done.4
  154.0 0.3 maximum_convert_fusion
  154.3 72.2 %reduce-scatter.5.cloned.1.call-done = f32[1024,768]{1,0:T(8,128)} async-done(((f32[1024,1536]{1,0:T(8,128)}), f32[1024,768]{1,0:T(8,128)}) %reduce-scatter.5.cloned.1.call-update) | async-done | bytes 3145744 | tf_op jit(solution)/shard_map/reduce_scatter | solution.py:72
  226.5 4.5 fusion.5
  231.1 1.4 collective-permute-start.7
  232.5 3.0 collective-permute-start.6
  235.6 0.9 collective-permute-done.6
  236.4 0.3 maximum_convert_fusion.1
  236.7 0.8 fusion.27
  237.5 1.2 copy-done.2
  238.8 6.2 fusion.42
  245.0 0.0 reduce-scatter.7.cloned.1.call-update
  245.0 0.0 all-gather.8.cloned.1.call-start
  245.1 3.2 multiply_convert_fusion
  248.3 0.2 reduce-scatter.9.cloned.1.call-start
  248.5 83.9 %reduce-scatter.7.cloned.1.call-done = f32[1024,768]{1,0:T(8,128)} async-done(((f32[1024,1536]{1,0:T(8,128)}), f32[1024,768]{1,0:T(8,128)}) %reduce-scatter.7.cloned.1.call-update) | async-done | bytes 3145744 | tf_op jit(solution)/shard_map/reduce_scatter | solution.py:72
  332.4 2.7 fusion.11
  335.1 1.4 collective-permute-start.9
  336.6 3.0 collective-permute-start.8
  339.6 0.8 collective-permute-done.8
  340.4 0.3 maximum_convert_fusion.4
  340.8 1.0 fusion.23
  341.8 6.9 fusion.46
  348.7 0.0 reduce-scatter.9.cloned.1.call-update
  348.8 0.0 reduce-scatter.11.cloned.1.call-start
  348.8 6.7 multiply_bitcast_fusion.1
  355.5 27.4 %all-gather.8.cloned.1.call-done = bf16[1024,1536]{1,0:T(8,128)(2,1)} async-done(((bf16[1024,768]{1,0:T(8,128)(2,1)}), bf16[1024,1536]{1,0:T(8,128)(2,1)}) %all-gather.8.cloned.1.call-update) | async-done | bytes 3145744 | tf_op jit(solution)/shard_map/all_gather | solution.py:46
  382.9 7.4 multiply_bitcast_fusion
  390.3 4.3 multiply_bitcast_fusion.2
  394.6 11.1 %pad_maximum_fusion = f32[3,1536,768]{2,1,0:T(8,128)} fusion(f32[1,1536,768]{2,1,0:T(8,128)} %multiply_bitcast_fusion, f32[1,1536,768]{2,1,0:T(8,128)} %multiply_bitcast_fusion.1, f32[1,1536,768]{2,1,0:T(8,128)} %multiply_bitcast_fusion.2), kind=kLoop, calls=%fused_computation | loop fusion | flops 7077888 | bytes 28311552 | tf_op jit(solution)/shard_map/stack | solution.py:86
  405.7 0.0 reduce-scatter.11.cloned.1.call-update
  405.7 60.0 %reduce-scatter.9.cloned.1.call-done = f32[1024,768]{1,0:T(8,128)} async-done(((f32[1024,1536]{1,0:T(8,128)}), f32[1024,768]{1,0:T(8,128)}) %reduce-scatter.9.cloned.1.call-update) | async-done | bytes 3145744 | tf_op jit(solution)/shard_map/reduce_scatter | solution.py:72
  465.7 2.9 fusion.17
  468.6 1.5 collective-permute-start.11
  470.1 2.8 collective-permute-start.10
  473.0 5.3 add_convert_fusion
  478.3 0.3 maximum_convert_fusion.5
  478.7 1.0 copy-done.5
  479.7 2.3 fusion.19
  482.1 294.4 %reduce-scatter.11.cloned.1.call-done = f32[3,24,768]{2,1,0:T(8,128)} async-done(((f32[3,1536,768]{2,1,0:T(8,128)}), f32[3,24,768]{2,1,0:T(8,128)}) %reduce-scatter.11.cloned.1.call-update) | async-done | bytes 221200 | tf_op jit(solution)/shard_map/reduce_scatter | solution.py:86
  (39 shorter events, 0.2 us)
Async XLA Ops:
  7.2 68.2 %all-gather.4.cloned.1.call-start = ((), (), s32[]{:S(2)}) async-start(), calls=%async_computation.4 | async-start | bytes 4718592 | tf_op jit(solution)/shard_map/all_gather | solution.py:46
  8.1 5.3 collective-permute-start.1
  9.4 4.0 collective-permute-start
  15.1 60.2 %copy-start.8 = (bf16[4,256,768]{2,1,0:T(8,128)(2,1)S(1)}, bf16[4,256,768]{2,1,0:T(8,128)(2,1)}, u32[]{:S(2)}) copy-start(bf16[4,256,768]{2,1,0:T(8,128)(2,1)} %param.4) | copy-start | bytes 4718596
  18.1 125.4 %all-gather.6.cloned.1.call-start = ((), (), s32[]{:S(2)}) async-start(), calls=%async_computation.5 | async-start | bytes 4718592 | tf_op jit(solution)/shard_map/all_gather | solution.py:46
  80.6 4.3 collective-permute-start.3
  81.9 3.9 collective-permute-start.2
  86.1 3.0 copy-start.9
  89.0 137.5 %reduce-scatter.5.cloned.1.call-start = ((), (), s32[]{:S(2)}) async-start(), calls=%async_computation.7 | async-start | bytes 9437184 | tf_op jit(solution)/shard_map/reduce_scatter | solution.py:72
  95.3 237.0 %reduce-scatter.7.cloned.1.call-start = ((), (), s32[]{:S(2)}) async-start(), calls=%async_computation.8 | async-start | bytes 9437184 | tf_op jit(solution)/shard_map/reduce_scatter | solution.py:72
  148.8 5.2 copy-start.6
  148.8 4.3 collective-permute-start.5
  150.1 3.9 collective-permute-start.4
  231.1 5.6 copy-start.10
  231.1 4.5 collective-permute-start.7
  232.5 3.9 collective-permute-start.6
  237.5 1.2 copy-start.2
  245.0 137.9 %all-gather.8.cloned.1.call-start = ((), (), s32[]{:S(2)}) async-start(), calls=%async_computation.6 | async-start | bytes 4718592 | tf_op jit(solution)/shard_map/all_gather | solution.py:46
  245.0 87.3 %copy-start.1 = (f32[4,256,768]{2,1,0:T(8,128)S(1)}, f32[4,256,768]{2,1,0:T(8,128)}, u32[]{:S(2)}) copy-start(f32[4,256,768]{2,1,0:T(8,128)} %get-tuple-element.15) | copy-start | bytes 9437188
  248.3 217.4 %reduce-scatter.9.cloned.1.call-start = ((), (), s32[]{:S(2)}) async-start(), calls=%async_computation.9 | async-start | bytes 9437184 | tf_op jit(solution)/shard_map/reduce_scatter | solution.py:72
  335.1 5.7 copy-start.3
  335.1 4.5 collective-permute-start.9
  336.6 3.9 collective-permute-start.8
  341.8 48.5 %copy-start.4 = (bf16[4,256,768]{2,1,0:T(8,128)(2,1)}, bf16[4,256,768]{2,1,0:T(8,128)(2,1)S(1)}, u32[]{:S(2)}) copy-start(bf16[4,256,768]{2,1,0:T(8,128)(2,1)S(1)} %fusion.23) | copy-start | bytes 4718596
  348.8 427.7 %reduce-scatter.11.cloned.1.call-start = ((), (), s32[]{:S(2)}) async-start(), calls=%async_computation.10 | async-start | bytes 14376960 | tf_op jit(solution)/shard_map/reduce_scatter | solution.py:86
  382.9 7.4 copy-start.11
  405.7 60.0 %copy-start = (f32[4,256,768]{2,1,0:T(8,128)S(1)}, f32[4,256,768]{2,1,0:T(8,128)}, u32[]{:S(2)}) copy-start(f32[4,256,768]{2,1,0:T(8,128)} %get-tuple-element.17) | copy-start | bytes 9437188
  465.7 7.3 copy-start.7
  465.7 7.3 copy-start.12
  468.6 9.7 %collective-permute-start.11 = (bf16[4,2,768]{2,1,0:T(2,128)(2,1)S(1)}, bf16[4,2,768]{2,1,0:T(2,128)(2,1)S(1)}, u32[]{:S(2)}, u32[]{:S(2)}) collective-permute-start(bf16[4,2,768]{2,1,0:T(2,128)(2,1)S(1)} %get-tuple-element.19), channel_id=1, source_target_pairs={{2,0},{4,2},{6,4},{8,6},{10,8},{12,10},{14,12},{16,14},{18,16},{20... | collective-permute-start | bytes 36872 | tf_op jit(solution)/shard_map/ppermute | solution.py:18
  470.1 8.2 %collective-permute-start.10 = (bf16[4,2,768]{2,1,0:T(2,128)(2,1)S(1)}, bf16[4,2,768]{2,1,0:T(2,128)(2,1)S(1)}, u32[]{:S(2)}, u32[]{:S(2)}) collective-permute-start(bf16[4,2,768]{2,1,0:T(2,128)(2,1)S(1)} %get-tuple-element.18), channel_id=1, source_target_pairs={{0,2},{2,4},{4,6},{6,8},{8,10},{10,12},{12,14},{14,16},{16,18},{18... | collective-permute-start | bytes 36872 | tf_op jit(solution)/shard_map/ppermute | solution.py:15
  478.3 1.4 copy-start.5
Sparse Core Ops, SparseCore 0:
  18.2 57.0 all-gather.3
  89.2 54.3 all-gather.5
  146.0 80.5 reduce-scatter.4
  245.1 87.2 reduce-scatter.6
  334.4 48.4 all-gather.7
  385.1 80.5 reduce-scatter.8
  468.8 307.5 reduce-scatter.10
where the time goes:
time: 784 us; the launch traced here: 783 us
  waiting for transfers between devices  647 us (83%)
  matrix products  53.5 us (7%)
  other arithmetic  37.8 us (5%)
  starting transfers between devices  26.7 us (3%)
  between operations  14.5 us (2%)
    reduce_scatter x1, waiting for transfers between devices, on_device(): lax.psum_scatter(jnp.stack(grad_list), 'seq', scatter_dimension=1, tiled=...  294 us
    reduce_scatter x3, waiting for transfers between devices, on_device(): back = lax.psum_scatter(term, 'ch', scatter_dimension=1, tiled=True)  216 us
    all_gather x3, waiting for transfers between devices, mixing(): lax.all_gather(act.reshape(seqs * length, chans), 'ch', axis=1, tiled=True)  133 us
    dot_general x3, matrix products, on_device(): jnp.einsum('rj,cj->rc', flat, mixers[block], preferred_element_type=jnp.f...  19.3 us
    dot_general x3, matrix products, on_device(): jnp.einsum('rc,rj->cj', gathered, flat, preferred_element_type=jnp.float32)  18.4 us
    ppermute x6, starting transfers between devices, padded_2(): lax.ppermute(lax.slice_in_dim(block, block.shape[dim] - width, None, axis...  18 us
    dot_general x3, matrix products, mixing(): mixed = jnp.dot(gathered, mixer, preferred_element_type=jnp.float32)  15.8 us
  transfers between devices with their start and end apart: 19, of which 11 were waited for; matrix products, arithmetic and copies ran while one was open for 9% of the time, Pallas kernels for 0%

commit v1 on v0

--- a/solution.py
+++ b/solution.py
@@ -43,7 +43,12 @@
 
 def mixing(center, act, mixer):
     seqs, length, chans = act.shape
-    gathered = lax.all_gather(act.reshape(seqs * length, chans), "ch", axis=1, tiled=True)
+    gathered = jnp.concatenate(
+        lax.all_to_all(
+            jnp.stack([act.reshape(seqs * length, chans)] * lax.axis_size("ch")), "ch", 0, 0
+        ),
+        axis=1,
+    )
     mixed = jnp.dot(gathered, mixer, preferred_element_type=jnp.float32)
     result = (center.astype(jnp.float32) + mixed.reshape(seqs, length, chans)).astype(jnp.bfloat16)
     return (gathered, result)

time: 784 us -> 752 us (0.959)
  waiting for transfers between devices: 647 us -> 461 us
  blocking collectives: 0 us -> 117 us
  local copies, waits for them, and re-layouts: 4.22 us -> 31 us
  starting transfers between devices: 26.7 us -> 36.2 us
    all_gather x3 -> x0, waiting for transfers between devices: 133 us -> none  [mixing(): lax.all_gather(act.reshape(seqs * length, chans), 'ch', axis=1, tiled=True)]
    all_to_all x0 -> x2, blocking collectives: none -> 117 us  [mixing(): lax.all_to_all(jnp.stack([act.reshape(seqs * length, chans)] * lax.axis_s...]
    reduce_scatter x3, waiting for transfers between devices: 216 us -> 102 us  [on_device(): back = lax.psum_scatter(term, 'ch', scatter_dimension=1, tiled=True)]
    all_to_all x0 -> x1, waiting for transfers between devices: none -> 62.1 us  [mixing(): lax.all_to_all(jnp.stack([act.reshape(seqs * length, chans)] * lax.axis_s...]
    dot_general x0 -> x3, local copies, waits for them, and re-layouts: none -> 14 us  [mixing(): mixed = jnp.dot(gathered, mixer, preferred_element_type=jnp.float32)]
  transfers between devices with their start and end apart: 19 -> 17, of which waited for: 11 -> 9; matrix products, arithmetic and copies ran while one was open for 9% -> 11% of each run, Pallas kernels for 0% -> 0%
where the time goes in v1:
time: 752 us; the launch traced here: 751 us
  waiting for transfers between devices  461 us (61%)
  blocking collectives  117 us (16%)
  matrix products  55.2 us (7%)
  other arithmetic  36.6 us (5%)
  starting transfers between devices  36.2 us (5%)
  local copies, waits for them, and re-layouts  31 us (4%)
  between operations  14.2 us (2%)
    reduce_scatter x1, waiting for transfers between devices, on_device(): lax.psum_scatter(jnp.stack(grad_list), 'seq', scatter_dimension=1, tiled=...  293 us
    all_to_all x2, blocking collectives, mixing(): lax.all_to_all(jnp.stack([act.reshape(seqs * length, chans)] * lax.axis_s...  117 us
    reduce_scatter x3, waiting for transfers between devices, on_device(): back = lax.psum_scatter(term, 'ch', scatter_dimension=1, tiled=True)  102 us
    all_to_all x1, waiting for transfers between devices, mixing(): lax.all_to_all(jnp.stack([act.reshape(seqs * length, chans)] * lax.axis_s...  62.1 us
    ppermute x6, starting transfers between devices, padded_2(): lax.ppermute(lax.slice_in_dim(block, block.shape[dim] - width, None, axis...  22.2 us
    dot_general x3, matrix products, on_device(): jnp.einsum('rj,cj->rc', flat, mixers[block], preferred_element_type=jnp.f...  19.8 us
    dot_general x3, matrix products, on_device(): jnp.einsum('rc,rj->cj', gathered, flat, preferred_element_type=jnp.float32)  18.5 us
    dot_general x3, matrix products, mixing(): mixed = jnp.dot(gathered, mixer, preferred_element_type=jnp.float32)  16.9 us
  transfers between devices with their start and end apart: 17, of which 9 were waited for; matrix products, arithmetic and copies ran while one was open for 11% of the time, Pallas kernels for 0%

profile of v1, /device:TPU:0, one launch (start us, length us, event | category | flops | bytes accessed | tf_op | source)
XLA Modules:
  0.0 751.0 jit_solution(9603362228798752897)
XLA Ops:
  7.2 7.4 fusion.41
  14.7 1.3 copy-done.16
  16.1 1.3 collective-permute-start.1
  17.4 3.0 collective-permute-start
  20.5 0.7 collective-permute-done
  21.2 0.3 maximum_convert_fusion.2
  21.6 2.7 multiply_convert_fusion.2
  24.6 76.8 %all_to_all.15 = bf16[2,1024,768]{2,1,0:T(8,128)(2,1)S(1)} all-to-all(bf16[2,1024,768]{2,1,0:T(8,128)(2,1)S(1)} %pad_maximum_fusion.1), channel_id=1, replica_groups=mesh['seq'=64,'ch'=2] {'ch'}, dimensions={0} | all-to-all | bytes 6291456 | tf_op jit(solution)/shard_map/all_to_all | solution.py:47
  101.4 1.7 copy-done
  103.1 3.2 copy.27
  106.3 3.3 dot_general.33
  109.6 5.6 add_convert_fusion.2
  115.3 1.3 collective-permute-start.3
  116.6 3.0 collective-permute-start.2
  119.7 0.8 collective-permute-done.2
  120.5 0.3 maximum_convert_fusion.3
  120.8 2.7 multiply_convert_fusion.1
  123.5 0.7 copy.28
  124.3 0.3 pad_maximum_fusion.2
  124.6 40.1 %all_to_all.16 = bf16[2,1024,768]{1,2,0:T(8,128)(2,1)S(1)} all-to-all(bf16[2,1024,768]{1,2,0:T(8,128)(2,1)S(1)} %pad_maximum_fusion.2), channel_id=1, replica_groups=mesh['seq'=64,'ch'=2] {'ch'}, dimensions={0} | all-to-all | bytes 6291456 | tf_op jit(solution)/shard_map/all_to_all | solution.py:47
  164.6 4.3 reshape.84
  168.9 5.7 add_convert_fusion.1
  174.7 1.3 collective-permute-start.5
  176.0 3.9 collective-permute-start.4
  180.0 0.9 collective-permute-done.4
  180.8 0.3 maximum_convert_fusion
  181.1 4.6 fusion.5
  185.7 1.4 collective-permute-start.7
  187.1 6.2 collective-permute-start.6
  193.3 0.9 collective-permute-done.6
  194.2 0.3 maximum_convert_fusion.1
  194.5 0.8 fusion.27
  195.3 1.1 copy-done.9
  196.4 6.2 fusion.44
  202.7 95.2 %reduce-scatter.7.cloned.1.call-done = f32[1024,768]{1,0:T(8,128)} async-done(((f32[1024,1536]{1,0:T(8,128)}), f32[1024,768]{1,0:T(8,128)}) %reduce-scatter.7.cloned.1.call-update) | async-done | bytes 3145744 | tf_op jit(solution)/shard_map/reduce_scatter | solution.py:77
  297.9 2.7 fusion.11
  300.7 1.4 collective-permute-start.9
  302.2 3.0 collective-permute-start.8
  305.2 0.8 collective-permute-done.8
  306.0 0.3 maximum_convert_fusion.4
  306.4 1.0 fusion.23
  307.4 1.1 copy-done.6
  308.5 6.1 fusion.48
  314.7 1.9 copy-done.5
  316.6 1.5 multiply_convert_fusion
  318.0 1.7 copy.31
  319.7 1.9 pad_maximum_fusion.3
  321.7 5.5 all-to-all-start.2
  327.5 2.9 copy.26
  330.4 7.2 multiply_bitcast_fusion.1
  337.6 62.1 %all-to-all-done.2 = bf16[2,1024,768]{1,2,0:T(8,128)(2,1)} async-done(((bf16[2,1024,768]{1,2,0:T(8,128)(2,1)}), bf16[2,1024,768]{1,2,0:T(8,128)(2,1)}, u32[]{:S(2)}, u32[]{:S(2)}) %all-to-all-start.2) | async-done | bytes 3145760 | tf_op jit(solution)/shard_map/all_to_all | solution.py:47
  399.7 7.1 multiply_bitcast_fusion
  406.8 4.2 multiply_bitcast_fusion.2
  411.0 11.1 %pad_maximum_fusion = f32[3,1536,768]{2,1,0:T(8,128)} fusion(f32[1,1536,768]{2,1,0:T(8,128)} %multiply_bitcast_fusion, f32[1,1536,768]{2,1,0:T(8,128)} %multiply_bitcast_fusion.1, f32[1,1536,768]{2,1,0:T(8,128)} %multiply_bitcast_fusion.2), kind=kLoop, calls=%fused_computation | loop fusion | flops 7077888 | bytes 28311552 | tf_op jit(solution)/shard_map/stack | solution.py:91
  422.1 6.4 reshape.85
  428.5 6.5 reduce-scatter.9.cloned.1.call-done
  435.0 2.9 fusion.17
  437.9 1.3 collective-permute-start.11
  439.2 3.0 collective-permute-start.10
  442.3 5.5 add_convert_fusion
  447.8 0.3 maximum_convert_fusion.5
  448.1 1.0 copy-done.8
  449.2 2.3 fusion.19
  451.5 293.0 %reduce-scatter.11.cloned.1.call-done = f32[3,24,768]{2,1,0:T(8,128)} async-done(((f32[3,1536,768]{2,1,0:T(8,128)}), f32[3,24,768]{2,1,0:T(8,128)}) %reduce-scatter.11.cloned.1.call-update) | async-done | bytes 221200 | tf_op jit(solution)/shard_map/reduce_scatter | solution.py:91
  (58 shorter events, 1.0 us)
Async XLA Ops:
  7.2 174.0 %reduce-scatter.5.cloned.1.call-start = ((), (), s32[]{:S(2)}) async-start(), calls=%async_computation.7 | async-start | bytes 9437184 | tf_op jit(solution)/shard_map/reduce_scatter | solution.py:77
  14.7 1.4 copy-start.16
  14.7 5.8 copy-start.19
  14.7 283.3 %reduce-scatter.7.cloned.1.call-start = ((), (), s32[]{:S(2)}) async-start(), calls=%async_computation.8 | async-start | bytes 9437184 | tf_op jit(solution)/shard_map/reduce_scatter | solution.py:77
  16.1 4.4 collective-permute-start.1
  17.4 3.9 collective-permute-start
  101.4 1.7 copy-start
  115.3 8.3 %copy-start.15 = (bf16[4,256,768]{2,1,0:T(8,128)(2,1)}, bf16[4,256,768]{2,1,0:T(8,128)(2,1)S(1)}, u32[]{:S(2)}) copy-start(bf16[4,256,768]{2,1,0:T(8,128)(2,1)S(1)} %add_convert_fusion.2) | copy-start | bytes 4718596
  115.3 4.3 collective-permute-start.3
  116.6 3.9 collective-permute-start.2
  164.6 4.3 copy-start.3
  174.7 6.1 copy-start.13
  174.7 5.2 collective-permute-start.5
  176.0 4.8 collective-permute-start.4
  185.7 8.8 %copy-start.17 = (bf16[4,256,768]{2,1,0:T(8,128)(2,1)S(1)}, bf16[4,256,768]{2,1,0:T(8,128)(2,1)}, u32[]{:S(2)}) copy-start(bf16[4,256,768]{2,1,0:T(8,128)(2,1)} %param.7) | copy-start | bytes 4718596
  185.7 7.6 %collective-permute-start.7 = (bf16[4,8,768]{2,1,0:T(8,128)(2,1)S(1)}, bf16[4,8,768]{2,1,0:T(8,128)(2,1)S(1)}, u32[]{:S(2)}, u32[]{:S(2)}) collective-permute-start(bf16[4,8,768]{2,1,0:T(8,128)(2,1)S(1)} %get-tuple-element.23), channel_id=1, source_target_pairs={{2,0},{4,2},{6,4},{8,6},{10,8},{12,10},{14,12},{16,14},{18,16},{20... | collective-permute-start | bytes 147464 | tf_op jit(solution)/shard_map/ppermute | solution.py:18
  187.1 7.0 collective-permute-start.6
  195.3 1.1 copy-start.9
  202.6 95.3 %copy-start.4 = (f32[4,256,768]{2,1,0:T(8,128)S(1)}, f32[4,256,768]{2,1,0:T(8,128)}, u32[]{:S(2)}) copy-start(f32[4,256,768]{2,1,0:T(8,128)} %get-tuple-element.15) | copy-start | bytes 9437188
  202.7 232.4 %reduce-scatter.9.cloned.1.call-start = ((), (), s32[]{:S(2)}) async-start(), calls=%async_computation.9 | async-start | bytes 9437184 | tf_op jit(solution)/shard_map/reduce_scatter | solution.py:77
  300.7 5.7 copy-start.10
  300.7 4.5 collective-permute-start.9
  302.2 3.9 collective-permute-start.8
  307.4 1.1 copy-start.6
  314.7 1.9 copy-start.5
  321.6 5.8 copy-start.1
  321.7 78.0 %all-to-all-start.2 = ((bf16[2,1024,768]{1,2,0:T(8,128)(2,1)}), bf16[2,1024,768]{1,2,0:T(8,128)(2,1)}, u32[]{:S(2)}, u32[]{:S(2)}) async-start(bf16[2,1024,768]{1,2,0:T(8,128)(2,1)} %pad_maximum_fusion.3), calls=%async_computation.2 | async-start | bytes 6291456 | tf_op jit(solution)/shard_map/all_to_all | solution.py:47
  327.2 417.3 %reduce-scatter.11.cloned.1.call-start = ((), (), s32[]{:S(2)}) async-start(), calls=%async_computation.10 | async-start | bytes 14376960 | tf_op jit(solution)/shard_map/reduce_scatter | solution.py:91
  330.4 69.3 %copy-start.18 = (bf16[4,256,768]{2,1,0:T(8,128)(2,1)S(1)}, bf16[4,256,768]{2,1,0:T(8,128)(2,1)}, u32[]{:S(2)}) copy-start(bf16[4,256,768]{2,1,0:T(8,128)(2,1)} %param.7) | copy-start | bytes 4718596
  399.7 7.1 copy-start.7
  399.7 7.1 copy-start.12
  422.1 12.9 %copy-start.2 = (f32[4,256,768]{2,1,0:T(8,128)S(1)}, f32[4,256,768]{2,1,0:T(8,128)}, u32[]{:S(2)}) copy-start(f32[4,256,768]{2,1,0:T(8,128)} %get-tuple-element.17) | copy-start | bytes 9437188
  435.0 7.3 copy-start.11
  435.0 7.3 copy-start.14
  437.9 9.9 %collective-permute-start.11 = (bf16[4,2,768]{2,1,0:T(2,128)(2,1)S(1)}, bf16[4,2,768]{2,1,0:T(2,128)(2,1)S(1)}, u32[]{:S(2)}, u32[]{:S(2)}) collective-permute-start(bf16[4,2,768]{2,1,0:T(2,128)(2,1)S(1)} %get-tuple-element.19), channel_id=1, source_target_pairs={{2,0},{4,2},{6,4},{8,6},{10,8},{12,10},{14,12},{16,14},{18,16},{20... | collective-permute-start | bytes 36872 | tf_op jit(solution)/shard_map/ppermute | solution.py:18
  439.2 8.6 %collective-permute-start.10 = (bf16[4,2,768]{2,1,0:T(2,128)(2,1)S(1)}, bf16[4,2,768]{2,1,0:T(2,128)(2,1)S(1)}, u32[]{:S(2)}, u32[]{:S(2)}) collective-permute-start(bf16[4,2,768]{2,1,0:T(2,128)(2,1)S(1)} %get-tuple-element.18), channel_id=1, source_target_pairs={{0,2},{2,4},{4,6},{6,8},{8,10},{10,12},{12,14},{14,16},{16,18},{18... | collective-permute-start | bytes 36872 | tf_op jit(solution)/shard_map/ppermute | solution.py:15
  447.8 1.4 copy-start.8
Sparse Core Ops, SparseCore 0:
  14.8 117.2 reduce-scatter.4
  202.8 95.1 reduce-scatter.6
  314.8 120.1 reduce-scatter.8
  438.0 306.4 reduce-scatter.10
